TPU v7x, 32 devices: a whole 2x2x4 slice. The times are simulated.
32 devices in a mesh: freq: 2 (over x), row: 16 (over z, y, core).
Axes of the slice: x: 2, y: 2, z: 4, core: 2. Of those that a mesh axis runs over, the one named last changes fastest.
Arguments:
- data_real: bfloat16 [16384, 8192], P(('freq', 'row')), parts along dimension 0, may hold values from -6 to 6
- data_imag: bfloat16 [16384, 8192], P(('freq', 'row')), parts along dimension 0, may hold values from -6 to 6
- counts: int32 [8, 8], replicated, may hold values from 0 to 4
- source_cols: int32 [128], replicated, may hold values from 0 to 8191, as said below
Outputs:
- pred_real: float32 [16384, 128], P(('freq', 'row')), parts along dimension 0
- pred_imag: float32 [16384, 128], P(('freq', 'row')), parts along dimension 0
There are 2 independent parts, one for each index of `freq`. A program takes and returns all parts, laid end to end along the dimension named above; an argument that names none is the same for every part. Nothing has to cross between parts.
Inputs may be any that keep to these rules, and one draw needn't show every extreme that they name: `source_cols`: 128 distinct grid points; 0 and 8191 are always among them.
All inputs are finite; a program needn't handle non-finite values.
Results may differ from a plain program's by a relative error of at most 0.0029.
Values may be sent and summed in bfloat16 or wider, within the bound.
A program may use at most 128 MiB of HBM per device.

v0:
```python
import math
import jax
import jax.numpy as jnp
from jax import lax
from jax.sharding import PartitionSpec as P

TILES = 8


def tile_weights(counts, row_ids, width):
    tile = width // TILES
    onehot = (row_ids[:, None] // tile == jnp.arange(TILES, dtype=jnp.int32)[None, :]).astype(
        jnp.float32
    )
    table = counts.astype(jnp.float32)
    forward = jnp.dot(onehot, table, precision=lax.Precision.HIGHEST)
    backward = jnp.dot(onehot, table.T, precision=lax.Precision.HIGHEST)
    height = row_ids.shape[0]
    forward = jnp.broadcast_to(forward[:, :, None], (height, TILES, tile)).reshape(height, width)
    backward = jnp.broadcast_to(backward[:, :, None], (height, TILES, tile)).reshape(height, width)
    return (forward, backward)


def complex_pair(left_real, left_imag, right_real, right_imag, dims):
    dot_rr = lax.dot_general(left_real, right_real, dims, preferred_element_type=jnp.float32)
    dot_ii = lax.dot_general(left_imag, right_imag, dims, preferred_element_type=jnp.float32)
    dot_ri = lax.dot_general(left_real, right_imag, dims, preferred_element_type=jnp.float32)
    dot_ir = lax.dot_general(left_imag, right_real, dims, preferred_element_type=jnp.float32)
    return jnp.concatenate([dot_rr - dot_ii, dot_ri + dot_ir], axis=1)


def shards(data_real, data_imag, counts, source_cols):
    rows, width = data_real.shape
    mirror_real, mirror_imag = (
        lax.all_to_all(data_real, "row", split_axis=1, concat_axis=0, tiled=True),
        lax.all_to_all(data_imag, "row", split_axis=1, concat_axis=0, tiled=True),
    )
    row_ids = lax.axis_index("row") * rows + jnp.arange(rows, dtype=jnp.int32)
    forward, backward = tile_weights(counts, row_ids, width)
    denom = jnp.maximum(forward + backward, 1.0)
    sym_real = (
        (forward * data_real.astype(jnp.float32) + backward * mirror_real.T.astype(jnp.float32))
        / denom
    ).astype(jnp.bfloat16)
    sym_imag = (
        (forward * data_imag.astype(jnp.float32) + backward * mirror_imag.T.astype(jnp.float32))
        / denom
    ).astype(jnp.bfloat16)
    panel_real = jnp.take(sym_real, source_cols, axis=1)
    panel_imag = jnp.take(sym_imag, source_cols, axis=1)
    sources = source_cols.shape[0]
    factor = -1.0 / math.sqrt(width)
    piece_real = lax.all_gather(panel_real, "row", axis=0, tiled=True)
    piece_imag = lax.all_gather(panel_imag, "row", axis=0, tiled=True)
    summed = complex_pair(sym_real, sym_imag, piece_real, piece_imag, (((1,), (0,)), ((), ())))
    predicted = factor * summed
    return (predicted[:, :sources], predicted[:, sources:])


def solution(mesh):
    placed = (P(("freq", "row"), None), P(("freq", "row"), None), P(), P())
    return jax.shard_map(
        shards,
        mesh=mesh,
        in_specs=placed,
        out_specs=(P(("freq", "row"), None), P(("freq", "row"), None)),
        check_vma=False,
    )
```

profile of v0, /device:TPU:0, one launch (start us, length us, event | category | flops | bytes accessed | tf_op | source)
XLA Modules:
  0.0 530.0 jit_solution(13418963480100498488)
XLA Ops:
  7.2 7.5 %copy.17 = bf16[64,16,8,512]{3,2,0,1:T(8,128)(2,1)} copy(bf16[64,16,8,512]{3,2,1,0:T(8,128)(2,1)} %bitcast.68) | data formatting | bytes 16777216 | tf_op jit(solution)/shard_map/all_to_all | solution.py:35
  14.7 7.4 %all-to-all-start = ((bf16[512,16,512]{2,0,1:T(8,128)(2,1)}), bf16[512,16,512]{2,0,1:T(8,128)(2,1)}, u32[]{:S(2)}, u32[]{:S(2)}) async-start(bf16[512,16,512]{2,0,1:T(8,128)(2,1)} %bitcast.71), calls=%async_computation | async-start | bytes 16777216 | tf_op jit(solution)/shard_map/all_to_all | solution.py:35
  22.1 7.5 %copy.16 = bf16[64,16,8,512]{3,2,0,1:T(8,128)(2,1)} copy(bf16[64,16,8,512]{3,2,1,0:T(8,128)(2,1)} %bitcast.69) | data formatting | bytes 16777216 | tf_op jit(solution)/shard_map/all_to_all | solution.py:36
  29.7 143.2 %all-to-all-done = bf16[512,16,512]{2,0,1:T(8,128)(2,1)} async-done(((bf16[512,16,512]{2,0,1:T(8,128)(2,1)}), bf16[512,16,512]{2,0,1:T(8,128)(2,1)}, u32[]{:S(2)}, u32[]{:S(2)}) %all-to-all-start) | async-done | bytes 8388640 | tf_op jit(solution)/shard_map/all_to_all | solution.py:35
  172.8 36.5 %all-to-all-start.1 = ((bf16[512,16,512]{2,0,1:T(8,128)(2,1)}), bf16[512,16,512]{2,0,1:T(8,128)(2,1)}, u32[]{:S(2)}, u32[]{:S(2)}) async-start(bf16[512,16,512]{2,0,1:T(8,128)(2,1)} %bitcast.70), calls=%async_computation.1 | async-start | bytes 16777216 | tf_op jit(solution)/shard_map/all_to_all | solution.py:36
  209.5 12.0 %copy.6 = bf16[512,8192]{0,1:T(8,128)(2,1)} copy(bf16[512,8192]{1,0:T(8,128)(2,1)} %param.6) | data formatting | bytes 16777216 | tf_op args[0]
  221.5 11.5 %copy.8 = bf16[512,8192]{0,1:T(8,128)(2,1)} copy(bf16[512,8192]{1,0:T(8,128)(2,1)} %param.7) | data formatting | bytes 16777216 | tf_op args[1]
  233.0 0.3 fusion.7
  233.3 0.3 fusion.8
  233.7 126.5 %all-to-all-done.1 = bf16[512,16,512]{2,0,1:T(8,128)(2,1)} async-done(((bf16[512,16,512]{2,0,1:T(8,128)(2,1)}), bf16[512,16,512]{2,0,1:T(8,128)(2,1)}, u32[]{:S(2)}, u32[]{:S(2)}) %all-to-all-start.1) | async-done | bytes 8388640 | tf_op jit(solution)/shard_map/all_to_all | solution.py:36
  360.1 18.6 %fusion.2 = (bf16[512,8192]{0,1:T(8,128)(2,1)}, bf16[512,8192]{0,1:T(8,128)(2,1)}) fusion(bf16[512,8192]{0,1:T(8,128)(2,1)} %copy.6, f32[512,8]{0,1:T(8,128)S(1)} %fusion.7, f32[512,8]{0,1:T(8,128)S(1)} %fusion.8, bf16[512,16,512]{2,0,1:T(8,128)(2,1)} %all-to-all-done, bf16[512,16,512]{2,0,1:T(8,128)(2,1)} %all-to-all-done.1, bf16[512,8192]{0,1:T(8,128)(2,1)} %copy.8), kind=kLoop, calls=%fused_computation.9 | loop fusion | flops 67108864 | bytes 50364416 | tf_op jit(solution)/shard_map/convert_element_type | solution.py:44
  378.7 5.3 %gather_fusion = bf16[128,512]{1,0:T(8,128)(2,1)S(1)} fusion(bf16[512,8192]{0,1:T(8,128)(2,1)} %get-tuple-element.7, s32[1024]{0:T(1024)S(1)} %pad_clamp_fusion), kind=kCustom, calls=%fused_computation.clone | custom fusion | bytes 262656 | tf_op jit(solution)/shard_map/jit(_take)/gather | solution.py:49
  384.0 5.3 %gather_fusion.1 = bf16[128,512]{1,0:T(8,128)(2,1)S(1)} fusion(bf16[512,8192]{0,1:T(8,128)(2,1)} %get-tuple-element.8, s32[1024]{0:T(1024)S(1)} %pad_clamp_fusion), kind=kCustom, calls=%fused_computation.1.clone | custom fusion | bytes 262656 | tf_op jit(solution)/shard_map/jit(_take)/gather | solution.py:50
  389.3 0.8 select_bitcast_fusion.1
  390.2 0.2 all-gather.5.cloned.1.call-start
  390.4 0.5 all-gather.5.cloned.1.call-update
  390.9 72.4 %all-gather.3.cloned.1.call-done = bf16[8192,128]{0,1:T(8,128)(2,1)} async-done(((bf16[512,128]{0,1:T(8,128)(2,1)}), bf16[8192,128]{0,1:T(8,128)(2,1)}) %all-gather.3.cloned.1.call-update) | async-done | bytes 2097168 | tf_op jit(solution)/shard_map/all_gather | solution.py:53
  463.3 5.3 fusion.17
  468.6 37.6 %all-gather.5.cloned.1.call-done = bf16[8192,128]{0,1:T(8,128)(2,1)} async-done(((bf16[512,128]{0,1:T(8,128)(2,1)}), bf16[8192,128]{0,1:T(8,128)(2,1)}) %all-gather.5.cloned.1.call-update) | async-done | bytes 2097168 | tf_op jit(solution)/shard_map/all_gather | solution.py:54
  506.2 5.4 %fusion.18 = f32[512,128]{0,1:T(8,128)S(1)} fusion(bf16[8192,128]{0,1:T(8,128)(2,1)} %all-gather.5.cloned.1.call-done, bf16[512,8192]{0,1:T(8,128)(2,1)} %get-tuple-element.7), kind=kOutput, calls=%fused_computation.42 | convolution fusion | flops 1073741824 | bytes 10747904 | tf_op jit(solution)/shard_map/dot_general | solution.py:27
  511.6 4.9 convolution_subtract_fusion
  516.6 4.8 convolution_add_fusion
  521.5 0.8 copy.10
  522.3 0.8 copy.11
  (16 shorter events, 0.2 us)
Async XLA Ops:
  14.7 158.2 %all-to-all-start = ((bf16[512,16,512]{2,0,1:T(8,128)(2,1)}), bf16[512,16,512]{2,0,1:T(8,128)(2,1)}, u32[]{:S(2)}, u32[]{:S(2)}) async-start(bf16[512,16,512]{2,0,1:T(8,128)(2,1)} %bitcast.71), calls=%async_computation | async-start | bytes 16777216 | tf_op jit(solution)/shard_map/all_to_all | solution.py:35
  172.8 187.3 %all-to-all-start.1 = ((bf16[512,16,512]{2,0,1:T(8,128)(2,1)}), bf16[512,16,512]{2,0,1:T(8,128)(2,1)}, u32[]{:S(2)}, u32[]{:S(2)}) async-start(bf16[512,16,512]{2,0,1:T(8,128)(2,1)} %bitcast.70), calls=%async_computation.1 | async-start | bytes 16777216 | tf_op jit(solution)/shard_map/all_to_all | solution.py:36
  209.4 253.9 %all-gather.3.cloned.1.call-start = ((), (), s32[]{:S(2)}) async-start(), calls=%async_computation.2 | async-start | bytes 2228224 | tf_op jit(solution)/shard_map/all_gather | solution.py:53
  221.4 11.5 %copy-start.3 = (s32[128]{0:T(128)S(1)}, s32[128]{0:T(128)}, u32[]{:S(2)}) copy-start(s32[128]{0:T(128)} %param.9) | copy-start | bytes 1540
  221.5 11.6 %copy-start.2 = (s32[8,8]{1,0:T(8,128)S(1)}, s32[8,8]{1,0:T(8,128)}, u32[]{:S(2)}) copy-start(s32[8,8]{1,0:T(8,128)} %param.8) | copy-start | bytes 772
  390.2 116.0 %all-gather.5.cloned.1.call-start = ((), (), s32[]{:S(2)}) async-start(), calls=%async_computation.3 | async-start | bytes 2228224 | tf_op jit(solution)/shard_map/all_gather | solution.py:54
  506.2 5.4 %copy-start.1 = (bf16[8192,128]{0,1:T(8,128)(2,1)S(1)}, bf16[8192,128]{0,1:T(8,128)(2,1)}, u32[]{:S(2)}) copy-start(bf16[8192,128]{0,1:T(8,128)(2,1)} %all-gather.5.cloned.1.call-done) | copy-start | bytes 6291460
  511.6 4.9 copy-start
Sparse Core Ops, SparseCore 0:
  390.3 72.9 all-gather.2
  466.0 40.1 all-gather.4
where the time goes:
time: 531 us; the launch traced here: 530 us
  waiting for transfers between devices  380 us (72%)
  local copies, waits for them, and re-layouts  50.9 us (10%)
  starting transfers between devices  44.2 us (8%)
  matrix products  21 us (4%)
  other arithmetic  19.4 us (4%)
  between operations  14.2 us (3%)
    all_to_all x1, waiting for transfers between devices, shards(): lax.all_to_all(data_real, 'row', split_axis=1, concat_axis=0, tiled=True)  143 us
    all_to_all x1, waiting for transfers between devices, shards(): lax.all_to_all(data_imag, 'row', split_axis=1, concat_axis=0, tiled=True)  126 us
    all_gather x1, waiting for transfers between devices, shards(): piece_real = lax.all_gather(panel_real, 'row', axis=0, tiled=True)  72.4 us
    all_gather x1, waiting for transfers between devices, shards(): piece_imag = lax.all_gather(panel_imag, 'row', axis=0, tiled=True)  37.6 us
    all_to_all x1, starting transfers between devices, shards(): lax.all_to_all(data_imag, 'row', split_axis=1, concat_axis=0, tiled=True)  36.5 us
    unnamed x12, local copies, waits for them, and re-layouts  25.2 us
    convert_element_type x1, other arithmetic, shards(): sym_real = ((forward * data_real.astype(jnp.float32) + backward * mirror_...  18.6 us
  transfers between devices with their start and end apart: 4, of which 4 were waited for; matrix products, arithmetic and copies ran while one was open for 7% of the time, Pallas kernels for 0%

commit v1 on v0

--- a/solution.py
+++ b/solution.py
@@ -50,8 +50,13 @@
     panel_imag = jnp.take(sym_imag, source_cols, axis=1)
     sources = source_cols.shape[0]
     factor = -1.0 / math.sqrt(width)
-    piece_real = lax.all_gather(panel_real, "row", axis=0, tiled=True)
-    piece_imag = lax.all_gather(panel_imag, "row", axis=0, tiled=True)
+    piece_real, piece_imag = jnp.split(
+        lax.all_gather(
+            jnp.concatenate([panel_real, panel_imag], axis=1), "row", axis=0, tiled=True
+        ),
+        [panel_real.shape[1]],
+        axis=1,
+    )
     summed = complex_pair(sym_real, sym_imag, piece_real, piece_imag, (((1,), (0,)), ((), ())))
     predicted = factor * summed
     return (predicted[:, :sources], predicted[:, sources:])

time: 531 us -> 499 us (0.940)
  waiting for transfers between devices: 380 us -> 355 us
  matrix products: 21 us -> 14.1 us
    all_gather x2 -> x1, waiting for transfers between devices: 110 us -> 85.2 us  [shards(): lax.all_gather(jnp.concatenate([panel_real, panel_imag], axis=1), 'row',...]
    unnamed x12 -> x18, local copies, waits for them, and re-layouts: 25.2 us -> 25.7 us
  transfers between devices with their start and end apart: 4 -> 3, of which waited for: 4 -> 3; matrix products, arithmetic and copies ran while one was open for 7% -> 6% of each run, Pallas kernels for 0% -> 0%
where the time goes in v1:
time: 499 us; the launch traced here: 498 us
  waiting for transfers between devices  355 us (71%)
  local copies, waits for them, and re-layouts  51.5 us (10%)
  starting transfers between devices  44 us (9%)
  other arithmetic  19.4 us (4%)
  between operations  14.2 us (3%)
  matrix products  14.1 us (3%)
    all_to_all x1, waiting for transfers between devices, shards(): lax.all_to_all(data_real, 'row', split_axis=1, concat_axis=0, tiled=True)  143 us
    all_to_all x1, waiting for transfers between devices, shards(): lax.all_to_all(data_imag, 'row', split_axis=1, concat_axis=0, tiled=True)  126 us
    all_gather x1, waiting for transfers between devices, shards(): lax.all_gather(jnp.concatenate([panel_real, panel_imag], axis=1), 'row',...  85.2 us
    all_to_all x1, starting transfers between devices, shards(): lax.all_to_all(data_imag, 'row', split_axis=1, concat_axis=0, tiled=True)  36.5 us
    unnamed x18, local copies, waits for them, and re-layouts  25.7 us
    convert_element_type x1, other arithmetic, shards(): sym_imag = ((forward * data_imag.astype(jnp.float32) + backward * mirror_...  18.6 us
  transfers between devices with their start and end apart: 3, of which 3 were waited for; matrix products, arithmetic and copies ran while one was open for 6% of the time, Pallas kernels for 0%

profile of v1, /device:TPU:0, one launch (start us, length us, event | category | flops | bytes accessed | tf_op | source)
XLA Modules:
  0.0 498.0 jit_solution(15915543845471990008)
XLA Ops:
  7.2 7.5 %copy.17 = bf16[64,16,8,512]{3,2,0,1:T(8,128)(2,1)} copy(bf16[64,16,8,512]{3,2,1,0:T(8,128)(2,1)} %bitcast.68) | data formatting | bytes 16777216 | tf_op jit(solution)/shard_map/all_to_all | solution.py:35
  14.7 7.4 %all-to-all-start = ((bf16[512,16,512]{2,0,1:T(8,128)(2,1)}), bf16[512,16,512]{2,0,1:T(8,128)(2,1)}, u32[]{:S(2)}, u32[]{:S(2)}) async-start(bf16[512,16,512]{2,0,1:T(8,128)(2,1)} %bitcast.71), calls=%async_computation | async-start | bytes 16777216 | tf_op jit(solution)/shard_map/all_to_all | solution.py:35
  22.1 7.5 %copy.16 = bf16[64,16,8,512]{3,2,0,1:T(8,128)(2,1)} copy(bf16[64,16,8,512]{3,2,1,0:T(8,128)(2,1)} %bitcast.69) | data formatting | bytes 16777216 | tf_op jit(solution)/shard_map/all_to_all | solution.py:36
  29.7 143.2 %all-to-all-done = bf16[512,16,512]{2,0,1:T(8,128)(2,1)} async-done(((bf16[512,16,512]{2,0,1:T(8,128)(2,1)}), bf16[512,16,512]{2,0,1:T(8,128)(2,1)}, u32[]{:S(2)}, u32[]{:S(2)}) %all-to-all-start) | async-done | bytes 8388640 | tf_op jit(solution)/shard_map/all_to_all | solution.py:35
  172.8 36.5 %all-to-all-start.1 = ((bf16[512,16,512]{2,0,1:T(8,128)(2,1)}), bf16[512,16,512]{2,0,1:T(8,128)(2,1)}, u32[]{:S(2)}, u32[]{:S(2)}) async-start(bf16[512,16,512]{2,0,1:T(8,128)(2,1)} %bitcast.70), calls=%async_computation.1 | async-start | bytes 16777216 | tf_op jit(solution)/shard_map/all_to_all | solution.py:36
  209.4 11.6 %copy.6 = bf16[512,8192]{0,1:T(8,128)(2,1)} copy(bf16[512,8192]{1,0:T(8,128)(2,1)} %param.6) | data formatting | bytes 16777216 | tf_op args[0]
  221.0 12.0 %copy.8 = bf16[512,8192]{0,1:T(8,128)(2,1)} copy(bf16[512,8192]{1,0:T(8,128)(2,1)} %param.7) | data formatting | bytes 16777216 | tf_op args[1]
  233.1 0.3 fusion.21
  233.4 0.3 fusion.22
  233.7 126.4 %all-to-all-done.1 = bf16[512,16,512]{2,0,1:T(8,128)(2,1)} async-done(((bf16[512,16,512]{2,0,1:T(8,128)(2,1)}), bf16[512,16,512]{2,0,1:T(8,128)(2,1)}, u32[]{:S(2)}, u32[]{:S(2)}) %all-to-all-start.1) | async-done | bytes 8388640 | tf_op jit(solution)/shard_map/all_to_all | solution.py:36
  360.1 18.6 %fusion.5 = (bf16[512,8192]{0,1:T(8,128)(2,1)}, bf16[512,8192]{0,1:T(8,128)(2,1)}) fusion(bf16[512,8192]{0,1:T(8,128)(2,1)} %copy.8, f32[512,8]{0,1:T(8,128)S(1)} %fusion.21, f32[512,8]{0,1:T(8,128)S(1)} %fusion.22, bf16[512,16,512]{2,0,1:T(8,128)(2,1)} %all-to-all-done.1, bf16[512,16,512]{2,0,1:T(8,128)(2,1)} %all-to-all-done, bf16[512,8192]{0,1:T(8,128)(2,1)} %copy.6), kind=kLoop, calls=%fused_computation.12 | loop fusion | flops 67108864 | bytes 50364416 | tf_op jit(solution)/shard_map/convert_element_type | solution.py:48
  378.6 5.3 %gather_fusion = bf16[128,512]{1,0:T(8,128)(2,1)S(1)} fusion(bf16[512,8192]{0,1:T(8,128)(2,1)} %get-tuple-element.8, s32[1024]{0:T(1024)S(1)} %pad_clamp_fusion), kind=kCustom, calls=%fused_computation.clone | custom fusion | bytes 262656 | tf_op jit(solution)/shard_map/jit(_take)/gather | solution.py:49
  384.0 5.3 %gather_fusion.1 = bf16[128,512]{1,0:T(8,128)(2,1)S(1)} fusion(bf16[512,8192]{0,1:T(8,128)(2,1)} %get-tuple-element.7, s32[1024]{0:T(1024)S(1)} %pad_clamp_fusion), kind=kCustom, calls=%fused_computation.1.clone | custom fusion | bytes 262656 | tf_op jit(solution)/shard_map/jit(_take)/gather | solution.py:50
  389.3 0.1 select_bitcast_fusion.1
  389.4 0.7 pad_maximum_fusion
  390.2 85.2 %all-gather.2.cloned.1.call-done = bf16[8192,256]{0,1:T(8,128)(2,1)} async-done(((bf16[512,256]{0,1:T(8,128)(2,1)}), bf16[8192,256]{0,1:T(8,128)(2,1)}) %all-gather.2.cloned.1.call-update) | async-done | bytes 4194320 | tf_op jit(solution)/shard_map/all_gather | solution.py:54
  475.4 5.4 %fusion.7 = f32[512,128]{0,1:T(8,128)S(1)} fusion(bf16[512,8192]{0,1:T(8,128)(2,1)} %get-tuple-element.7, bf16[8192,256]{0,1:T(8,128)(2,1)} %all-gather.2.cloned.1.call-done), kind=kOutput, calls=%fused_computation.16 | convolution fusion | flops 1073741824 | bytes 10747904 | tf_op jit(solution)/shard_map/dot_general | solution.py:26
  480.8 5.6 %fusion.9 = f32[512,128]{0,1:T(8,128)S(1)} fusion(bf16[512,8192]{0,1:T(8,128)(2,1)} %get-tuple-element.8, bf16[8192,256]{0,1:T(8,128)(2,1)S(1)} %copy-done), kind=kOutput, calls=%fused_computation.18 | convolution fusion | flops 1073741824 | bytes 10747904 | tf_op jit(solution)/shard_map/dot_general | solution.py:27
  486.4 0.4 slice-done.3
  486.8 1.3 fusion.18
  488.1 1.3 fusion.15
  489.4 0.1 maximum_multiply_fusion
  489.5 0.8 copy.10
  490.3 0.8 copy.11
  (22 shorter events, 0.1 us)
Async XLA Ops:
  14.7 158.2 %all-to-all-start = ((bf16[512,16,512]{2,0,1:T(8,128)(2,1)}), bf16[512,16,512]{2,0,1:T(8,128)(2,1)}, u32[]{:S(2)}, u32[]{:S(2)}) async-start(bf16[512,16,512]{2,0,1:T(8,128)(2,1)} %bitcast.71), calls=%async_computation | async-start | bytes 16777216 | tf_op jit(solution)/shard_map/all_to_all | solution.py:35
  172.8 187.3 %all-to-all-start.1 = ((bf16[512,16,512]{2,0,1:T(8,128)(2,1)}), bf16[512,16,512]{2,0,1:T(8,128)(2,1)}, u32[]{:S(2)}, u32[]{:S(2)}) async-start(bf16[512,16,512]{2,0,1:T(8,128)(2,1)} %bitcast.70), calls=%async_computation.1 | async-start | bytes 16777216 | tf_op jit(solution)/shard_map/all_to_all | solution.py:36
  209.4 266.0 %all-gather.2.cloned.1.call-start = ((), (), s32[]{:S(2)}) async-start(), calls=%async_computation.2 | async-start | bytes 4456448 | tf_op jit(solution)/shard_map/all_gather | solution.py:54
  221.0 12.0 %copy-start.2 = (s32[128]{0:T(128)S(1)}, s32[128]{0:T(128)}, u32[]{:S(2)}) copy-start(s32[128]{0:T(128)} %param.9) | copy-start | bytes 1540
  221.0 12.1 %copy-start.1 = (s32[8,8]{1,0:T(8,128)S(1)}, s32[8,8]{1,0:T(8,128)}, u32[]{:S(2)}) copy-start(s32[8,8]{1,0:T(8,128)} %param.8) | copy-start | bytes 772
  475.3 5.4 %copy-start = (bf16[8192,256]{0,1:T(8,128)(2,1)S(1)}, bf16[8192,256]{0,1:T(8,128)(2,1)}, u32[]{:S(2)}) copy-start(bf16[8192,256]{0,1:T(8,128)(2,1)} %all-gather.2.cloned.1.call-done) | copy-start | bytes 12582916
  475.3 11.0 %slice-start.2 = ((s8[8388608]{0:T(1024)(128)(4,1)}), s8[4194304]{0:T(1024)(128)(4,1)S(1)}, s32[]{:S(2)}) async-start(s8[8388608]{0:T(1024)(128)(4,1)} %bitcast.66), calls=%async_computation.5 | async-start | bytes 8388608
  475.3 12.7 %slice-start = ((s8[8388608]{0:T(1024)(128)(4,1)}), s8[4194304]{0:T(1024)(128)(4,1)S(1)}, s32[]{:S(2)}) async-start(s8[8388608]{0:T(1024)(128)(4,1)} %bitcast.64), calls=%async_computation.3 | async-start | bytes 8388608
  480.8 6.0 %slice-start.3 = ((s8[8388608]{0:T(1024)(128)(4,1)}), s8[4194304]{0:T(1024)(128)(4,1)S(1)}, s32[]{:S(2)}) async-start(s8[8388608]{0:T(1024)(128)(4,1)} %bitcast.66), calls=%async_computation.6 | async-start | bytes 8388608
  480.8 7.3 %slice-start.1 = ((s8[8388608]{0:T(1024)(128)(4,1)}), s8[4194304]{0:T(1024)(128)(4,1)S(1)}, s32[]{:S(2)}) async-start(s8[8388608]{0:T(1024)(128)(4,1)} %bitcast.64), calls=%async_computation.4 | async-start | bytes 8388608
Sparse Core Ops, SparseCore 0:
  390.3 85.0 all-gather.1
